TPU v7x, 32 devices: a whole 2x2x4 slice. The times are simulated.
32 devices in a mesh: group: 2 (over x), expert: 16 (over z, y, core).
Axes of the slice: x: 2, y: 2, z: 4, core: 2. Of those that a mesh axis runs over, the one named last changes fastest.
Arguments:
- rows: bfloat16 [4096, 1024], P(('group', 'expert')), parts along dimension 0, may hold values from -6 to 6
- cotangent: bfloat16 [4096, 1024], P(('group', 'expert')), parts along dimension 0, may hold values from -1.5 to 1.5
- up_proj: bfloat16 [1024, 65536], P(None, 'expert'), may hold values from -0.1875 to 0.1875
- down_proj: bfloat16 [65536, 1024], P('expert'), may hold values from -0.125 to 0.125
- mix_weight: float32 [8, 4], replicated, may hold values from 0.25 to 1
- task_counts: int32 [32, 8], P(('group', 'expert')), parts along dimension 0, may hold values from 1 to 18, 128 in all within a row
- expert_order: int32 [32, 32], P(('group', 'expert')), parts along dimension 0, may hold values from 0 to 31, each once within a row
Outputs:
- mixed: bfloat16 [4096, 1024], P(('group', 'expert')), parts along dimension 0
- row_gradient: bfloat16 [4096, 1024], P(('group', 'expert')), parts along dimension 0
- up_grad: bfloat16 [2048, 65536], P('group', 'expert'), parts along dimension 0
- down_grad: bfloat16 [65536, 2048], P('expert', 'group'), parts along dimension 1
There are 2 independent parts, one for each index of `group`. A program takes and returns all parts, laid end to end along the dimension named above; an argument that names none is the same for every part. Nothing has to cross between parts.
Inputs may be any that keep to these rules, and one draw needn't show every extreme that they name: `task_counts`: in each block the 8 counts sum to 128, and one of them is exactly 18. Each row of expert_order names every expert once.
All inputs are finite; a program needn't handle non-finite values.
Results may differ from a plain program's by a relative error of at most 0.0085.
Values may be sent and summed in bfloat16 or wider, within the bound.
A program may use at most 128 MiB of HBM per device.

v0:
```python
import jax
import jax.numpy as jnp
from jax import lax
from jax.sharding import PartitionSpec as P

FF = 2048
EXPERTS = 32
TASKS = 8
K = 4
CAP = 18


def block_route(counts, expert_list, mix_flat, row_total):
    firsts = jnp.cumsum(counts) - counts
    labels = jnp.arange(EXPERTS, dtype=jnp.int32)
    matches = expert_list[None, :] == labels[:, None]
    position = jnp.sum(jnp.where(matches, labels[None, :], 0), axis=1)
    task_of = position // K
    task_match = task_of[:, None] == jnp.arange(TASKS, dtype=jnp.int32)[None, :]
    count_of = jnp.sum(jnp.where(task_match, counts[None, :], 0), axis=1)
    first_of = jnp.sum(jnp.where(task_match, firsts[None, :], 0), axis=1)
    weight_of = jnp.sum(
        jnp.where(matches, mix_flat[None, :], jnp.zeros_like(mix_flat)[None, :]), axis=1
    )
    slot_index = jnp.arange(CAP, dtype=jnp.int32)
    filled = slot_index[None, :] < count_of[:, None]
    targets = first_of[:, None] + slot_index[None, :]
    row_index = jnp.arange(row_total, dtype=jnp.int32)
    selection_index = (targets[:, :, None] == row_index[None, None, :]) & filled[:, :, None]
    selection_index = selection_index.reshape(EXPERTS * CAP, row_total).astype(jnp.float32)
    slot_weight = jnp.where(filled, weight_of[:, None], jnp.zeros_like(weight_of)[:, None]).reshape(
        -1
    )
    return (selection_index, slot_weight)


def to_owners(values, copies, owners):
    if copies > 1:
        return jnp.repeat(values, copies, axis=0)
    return values.reshape((owners, -1) + values.shape[2:])


def from_owners(values, copies, hidden_width):
    if copies > 1:
        return jnp.sum(values.reshape(EXPERTS, copies, CAP, hidden_width), axis=1)
    return values.reshape(EXPERTS, CAP, hidden_width)


def forward_part(got_rows, up_local, down_local, owners, local_count, slot_count):
    hidden_width = got_rows.shape[-1]
    inputs = got_rows.reshape(owners, local_count, slot_count, hidden_width)
    pre = jnp.einsum("nlcd,dlf->nlcf", inputs, up_local, preferred_element_type=jnp.float32)
    act = jax.nn.silu(pre).astype(jnp.bfloat16)
    outputs = jnp.einsum("nlcf,lfd->nlcd", act, down_local, preferred_element_type=jnp.float32)
    return (inputs, pre, act, outputs.reshape(owners, local_count * slot_count, hidden_width))


def backward_part(
    inputs, got_grads, pre, act, up_local, down_local, owners, local_count, slot_count
):
    hidden_width = inputs.shape[-1]
    scaled = got_grads.reshape(owners, local_count, slot_count, hidden_width)
    act_grad = jnp.einsum("nlcd,lfd->nlcf", scaled, down_local, preferred_element_type=jnp.float32)
    sigmoid = jax.nn.sigmoid(pre)
    pre_grad = (act_grad * sigmoid * (1.0 + pre * (1.0 - sigmoid))).astype(jnp.bfloat16)
    down_grad = jnp.einsum("nlcf,nlcd->lfd", act, scaled, preferred_element_type=jnp.float32)
    up_grad = jnp.einsum("nlcd,nlcf->dlf", inputs, pre_grad, preferred_element_type=jnp.float32)
    partial_grads = jnp.einsum(
        "nlcf,dlf->nlcd", pre_grad, up_local, preferred_element_type=jnp.float32
    )
    units = up_local.shape[1] * up_local.shape[2]
    return (
        up_grad.reshape(hidden_width, units),
        down_grad.reshape(units, hidden_width),
        partial_grads.reshape(owners, local_count * slot_count, hidden_width),
    )


def per_device(rows, cotangent, up_proj, down_proj, mix_weight, task_counts, expert_order):
    owners = lax.axis_size("expert")
    row_total = rows.shape[0]
    hidden_width = rows.shape[1]
    units = up_proj.shape[1]
    local_units = min(units, FF)
    local_count = max(units // FF, 1)
    copies = max(FF // units, 1)
    selection_index, slot_weight = block_route(
        task_counts[0], expert_order[0], mix_weight.reshape(-1), row_total
    )
    select_half = selection_index.astype(jnp.bfloat16)
    slot_row_values = jnp.dot(select_half, rows, preferred_element_type=jnp.float32).astype(
        jnp.bfloat16
    )
    slot_gradient_rows = jnp.dot(select_half, cotangent, preferred_element_type=jnp.float32)
    scaled = (slot_weight[:, None] * slot_gradient_rows).astype(jnp.bfloat16)
    upper_bound = lax.Precision.HIGHEST
    sent_rows = to_owners(slot_row_values.reshape(EXPERTS, CAP, hidden_width), copies, owners)
    sent_grads = to_owners(scaled.reshape(EXPERTS, CAP, hidden_width), copies, owners)
    up_local = up_proj.reshape(hidden_width, local_count, local_units)
    down_local = down_proj.reshape(local_count, local_units, hidden_width)
    got_rows = lax.all_to_all(sent_rows, "expert", split_axis=0, concat_axis=0, tiled=True)
    inputs, pre, act, outputs = forward_part(
        got_rows, up_local, down_local, owners, local_count, CAP
    )
    back_out = lax.all_to_all(outputs, "expert", split_axis=0, concat_axis=0, tiled=True)
    got_grads = lax.all_to_all(sent_grads, "expert", split_axis=0, concat_axis=0, tiled=True)
    up_full, down_full, partial_grads = backward_part(
        inputs, got_grads, pre, act, up_local, down_local, owners, local_count, CAP
    )
    back_grads = lax.all_to_all(partial_grads, "expert", split_axis=0, concat_axis=0, tiled=True)
    up_grad = up_full.astype(jnp.bfloat16)
    down_grad = down_full.astype(jnp.bfloat16)
    returned = from_owners(back_out, copies, hidden_width).reshape(EXPERTS * CAP, hidden_width)
    summed_grads = from_owners(back_grads, copies, hidden_width).reshape(
        EXPERTS * CAP, hidden_width
    )
    weighted_rows = returned * slot_weight[:, None]
    mixed = jnp.dot(selection_index.T, weighted_rows, precision=upper_bound).astype(jnp.bfloat16)
    row_gradient = jnp.dot(selection_index.T, summed_grads, precision=upper_bound).astype(
        jnp.bfloat16
    )
    return (mixed, row_gradient, up_grad, down_grad)


def solution(mesh):
    return jax.shard_map(
        per_device,
        mesh=mesh,
        in_specs=(
            P(("group", "expert"), None),
            P(("group", "expert"), None),
            P(None, "expert"),
            P("expert", None),
            P(),
            P(("group", "expert"), None),
            P(("group", "expert"), None),
        ),
        out_specs=(
            P(("group", "expert"), None),
            P(("group", "expert"), None),
            P("group", "expert"),
            P("expert", "group"),
        ),
        check_vma=False,
    )
```

profile of v0, /device:TPU:15, one launch (start us, length us, event | category | flops | bytes accessed | tf_op | source)
XLA Modules:
  0.0 211.1 jit_solution(2312489915676028029)
XLA Ops:
  0.6 0.0 copy-start
  0.6 0.8 select_reduce_fusion.1
  1.5 0.8 reduce-window_clone.1
  2.3 0.7 subtract_bitcast_fusion
  3.0 0.7 select_reduce_fusion.2
  3.7 0.1 iota_add_fusion
  3.8 0.1 add.38
  3.9 0.1 iota_compare_fusion.1
  4.0 0.1 lt.24
  4.1 0.0 copy-done
  4.1 0.5 convolution_convert_fusion
  4.6 1.2 reshape_reshape.12
  5.8 6.5 %all-to-all-start = ((bf16[16,36,1024]{2,1,0:T(8,128)(2,1)}), bf16[16,36,1024]{2,1,0:T(8,128)(2,1)S(1)}, u32[]{:S(2)}, u32[]{:S(2)}) async-start(bf16[16,36,1024]{2,1,0:T(8,128)(2,1)} %reshape_reshape.12), calls=%async_computation | async-start | bytes 2621440 | tf_op jit(solution)/shard_map/all_to_all | solution.py:101
  12.3 0.0 copy-start.7
  12.3 0.0 copy-start.5
  12.4 14.5 %reshape.120 = bf16[1024,2,2048]{2,1,0:T(2,128)(2,1)} reshape(bf16[1024,4096]{1,0:T(8,128)(2,1)} %param.9) | data formatting | bytes 16777216 | tf_op jit(solution)/shard_map/reshape | solution.py:99
  26.8 0.0 copy-done.6
  26.8 0.1 copy.48
  26.9 0.1 broadcast_in_dim.90
  27.0 0.0 copy-done.7
  27.0 0.1 select_reduce_fusion
  27.1 0.1 broadcast_in_dim.93
  27.2 0.1 broadcast_in_dim.94
  27.3 0.0 copy-done.5
  27.3 0.5 multiply_convert_fusion
  27.9 1.2 reshape_reshape.14
  29.1 13.8 %all-to-all-done = bf16[16,36,1024]{2,1,0:T(8,128)(2,1)S(1)} async-done(((bf16[16,36,1024]{2,1,0:T(8,128)(2,1)}), bf16[16,36,1024]{2,1,0:T(8,128)(2,1)S(1)}, u32[]{:S(2)}, u32[]{:S(2)}) %all-to-all-start) | async-done | bytes 1179680 | tf_op jit(solution)/shard_map/all_to_all | solution.py:101
  42.9 5.0 %all-to-all-start.2 = ((bf16[16,36,1024]{2,1,0:T(8,128)(2,1)}), bf16[16,36,1024]{2,1,0:T(8,128)(2,1)S(1)}, u32[]{:S(2)}, u32[]{:S(2)}) async-start(bf16[16,36,1024]{2,1,0:T(8,128)(2,1)} %reshape_reshape.14), calls=%async_computation.2 | async-start | bytes 2621440 | tf_op jit(solution)/shard_map/all_to_all | solution.py:106
  47.9 0.0 slice-start
  47.9 0.7 copy.43
  48.6 0.0 copy-start.3
  48.6 0.0 slice-start.1
  48.6 10.8 %fusion.2 = f32[2,16,18,2048]{3,2,1,0:T(8,128)S(1)} fusion(bf16[1024,2,2048,1]{2,1,0,3:T(2,128)(2,1)} %bitcast.66, bf16[16,2,18,1024]{3,0,2,1:T(8,128)(2,1)S(1)} %bitcast.69), kind=kOutput, calls=%fused_computation.4 | convolution fusion | flops 2415919104 | bytes 14286848 | tf_op jit(solution)/shard_map/nlcd,dlf->nlcf/dot_general | solution.py:52
  59.4 0.0 copy-done.3
  59.4 0.0 copy-start.8
  59.4 0.0 slice-done
  59.4 0.0 slice-done.1
  59.4 3.7 %convolution_bitcast_fusion = f32[16,2,18,1024]{3,2,0,1:T(8,128)S(1)} fusion(bf16[2,2048,1024,1]{2,1,3,0:T(8,128)(2,1)S(1)} %bitcast.77, f32[2,16,18,2048]{3,2,1,0:T(8,128)S(1)} %fusion.2), kind=kOutput, calls=%fused_computation.21 | convolution fusion | flops 2421817344 | bytes 15466496 | tf_op jit(solution)/shard_map/nlcf,lfd->nlcd/dot_general | solution.py:54
  63.1 0.0 copy-done.8
  63.1 1.4 copy.46
  64.5 2.9 %copy.47 = f32[16,36,1024]{2,1,0:T(8,128)} copy(f32[16,36,1024]{2,0,1:T(8,128)S(1)} %bitcast.64) | data formatting | bytes 4718592 | tf_op jit(solution)/shard_map/reshape | solution.py:55
  67.4 10.9 %all-to-all-done.2 = bf16[16,36,1024]{2,1,0:T(8,128)(2,1)S(1)} async-done(((bf16[16,36,1024]{2,1,0:T(8,128)(2,1)}), bf16[16,36,1024]{2,1,0:T(8,128)(2,1)S(1)}, u32[]{:S(2)}, u32[]{:S(2)}) %all-to-all-start.2) | async-done | bytes 1179680 | tf_op jit(solution)/shard_map/all_to_all | solution.py:106
  78.4 1.1 copy-done.2
  79.4 5.0 %all-to-all-start.1 = ((f32[16,36,1024]{2,1,0:T(8,128)}), f32[16,36,1024]{2,1,0:T(8,128)S(1)}, u32[]{:S(2)}, u32[]{:S(2)}) async-start(f32[16,36,1024]{2,1,0:T(8,128)} %copy.47), calls=%async_computation.1 | async-start | bytes 5242880 | tf_op jit(solution)/shard_map/all_to_all | solution.py:105
  84.4 2.0 copy.49
  86.4 0.0 copy-start.4
  86.4 11.9 %fusion.5 = bf16[16,2,18,2048]{3,2,0,1:T(8,128)(2,1)S(1)} fusion(f32[2,16,18,2048]{3,2,1,0:T(8,128)} %copy-done.8, bf16[2,2048,1024,1]{2,1,3,0:T(8,128)(2,1)} %bitcast.74, bf16[16,2,18,1024]{3,0,2,1:T(8,128)(2,1)S(1)} %bitcast.71), kind=kOutput, calls=%fused_computation.8 | convolution fusion | flops 2426535936 | bytes 16646144 | tf_op jit(solution)/shard_map/nlcd,lfd->nlcf/dot_general | solution.py:63
  98.3 0.0 copy-done.4
  98.3 0.0 copy-start.9
  98.3 13.0 %fusion.13 = f32[16,2,18,1024]{3,2,0,1:T(8,128)S(1)} fusion(bf16[16,2,18,2048]{3,2,0,1:T(8,128)(2,1)S(1)} %fusion.5, bf16[1024,2,2048,1]{2,1,0,3:T(2,128)(2,1)} %bitcast.67), kind=kOutput, calls=%fused_computation.20 | convolution fusion | flops 2415919104 | bytes 13107200 | tf_op jit(solution)/shard_map/nlcf,dlf->nlcd/dot_general | solution.py:68
  111.3 0.0 copy-done.9
  111.3 1.4 copy.52
  112.7 2.9 %copy.53 = f32[16,36,1024]{2,1,0:T(8,128)} copy(f32[16,36,1024]{2,0,1:T(8,128)S(1)} %bitcast.65) | data formatting | bytes 4718592 | tf_op jit(solution)/shard_map/reshape | solution.py:75
  115.6 27.4 %all-to-all-done.1 = f32[16,36,1024]{2,1,0:T(8,128)S(1)} async-done(((f32[16,36,1024]{2,1,0:T(8,128)}), f32[16,36,1024]{2,1,0:T(8,128)S(1)}, u32[]{:S(2)}, u32[]{:S(2)}) %all-to-all-start.1) | async-done | bytes 2359328 | tf_op jit(solution)/shard_map/all_to_all | solution.py:105
  143.0 5.2 %all-to-all-start.3 = ((f32[16,36,1024]{2,1,0:T(8,128)}), f32[16,36,1024]{2,1,0:T(8,128)}, u32[]{:S(2)}, u32[]{:S(2)}) async-start(f32[16,36,1024]{2,1,0:T(8,128)} %copy.53), calls=%async_computation.3 | async-start | bytes 5242880 | tf_op jit(solution)/shard_map/all_to_all | solution.py:110
  148.2 10.6 %bitcast_convert_fusion.1 = bf16[2,2048,1024]{2,1,0:T(8,128)(2,1)} fusion(bf16[16,2,18,2048]{3,2,0,1:T(8,128)(2,1)} %copy-done.9, bf16[16,2,18,1024]{3,0,2,1:T(8,128)(2,1)} %bitcast.70), kind=kOutput, calls=%fused_computation.1 | convolution fusion | flops 2420113408 | bytes 11927552 | tf_op jit(solution)/shard_map/nlcd,nlcf->dlf/dot_general | solution.py:67
  158.8 11.9 %copy.56 = bf16[1024,4096]{1,0:T(8,128)(2,1)} copy(bf16[1024,4096]{0,1:T(8,128)(2,1)} %bitcast.68) | data formatting | bytes 16777216
  170.7 12.1 %bitcast_convert_fusion = bf16[2,2048,1024]{2,1,0:T(8,128)(2,1)} fusion(bf16[16,2,18,1024]{3,0,2,1:T(8,128)(2,1)} %bitcast.72, f32[2,16,18,2048]{3,2,1,0:T(8,128)} %copy-done.8), kind=kOutput, calls=%fused_computation | convolution fusion | flops 2426011648 | bytes 14286848 | tf_op jit(solution)/shard_map/nlcf,nlcd->lfd/dot_general | solution.py:66
  182.8 1.5 reshape_reshape.13
  184.3 3.7 %fusion.20 = bf16[128,1024]{1,0:T(8,128)(2,1)} fusion(f32[576,1024]{1,0:T(8,128)} %reshape_reshape.13, f32[576]{0:T(1024)S(1)} %broadcast_select_fusion, s32[576]{0:T(1024)S(1)} %add.38, pred[576]{0:T(1024)(128)(4,1)S(1)} %lt.24), kind=kOutput, calls=%fused_computation.28 | convolution fusion | flops 906838016 | bytes 2626624 | tf_op jit(solution)/shard_map/dot_general | solution.py:118
  188.1 18.7 %all-to-all-done.3 = f32[16,36,1024]{2,1,0:T(8,128)} async-done(((f32[16,36,1024]{2,1,0:T(8,128)}), f32[16,36,1024]{2,1,0:T(8,128)}, u32[]{:S(2)}, u32[]{:S(2)}) %all-to-all-start.3) | async-done | bytes 2359328 | tf_op jit(solution)/shard_map/all_to_all | solution.py:110
  206.8 1.8 reshape_reshape.15
  208.6 2.0 convolution_convert_fusion.1
  210.6 0.0 copy-done.1
  (6 shorter events, 0.0 us)
Async XLA Ops:
  0.6 3.4 %copy-start = (bf16[128,1024]{1,0:T(8,128)(2,1)S(1)}, bf16[128,1024]{1,0:T(8,128)(2,1)}, u32[]{:S(2)}) copy-start(bf16[128,1024]{1,0:T(8,128)(2,1)} %param.7) | copy-start | bytes 786436
  5.8 37.1 %all-to-all-start = ((bf16[16,36,1024]{2,1,0:T(8,128)(2,1)}), bf16[16,36,1024]{2,1,0:T(8,128)(2,1)S(1)}, u32[]{:S(2)}, u32[]{:S(2)}) async-start(bf16[16,36,1024]{2,1,0:T(8,128)(2,1)} %reshape_reshape.12), calls=%async_computation | async-start | bytes 2621440 | tf_op jit(solution)/shard_map/all_to_all | solution.py:101
  12.3 14.5 %copy-start.6 = (f32[8,4]{0,1:T(4,128)S(1)}, f32[8,4]{0,1:T(4,128)}, u32[]{:S(2)}) copy-start(f32[8,4]{0,1:T(4,128)} %param.11) | copy-start | bytes 388
  12.3 14.7 %copy-start.7 = (s32[1,32]{1,0:T(1,128)S(1)}, s32[1,32]{1,0:T(1,128)}, u32[]{:S(2)}) copy-start(s32[1,32]{1,0:T(1,128)} %param.13) | copy-start | bytes 388
  12.3 15.0 %copy-start.5 = (bf16[128,1024]{1,0:T(8,128)(2,1)S(1)}, bf16[128,1024]{1,0:T(8,128)(2,1)}, u32[]{:S(2)}) copy-start(bf16[128,1024]{1,0:T(8,128)(2,1)} %param.8) | copy-start | bytes 786436
  42.9 35.5 %all-to-all-start.2 = ((bf16[16,36,1024]{2,1,0:T(8,128)(2,1)}), bf16[16,36,1024]{2,1,0:T(8,128)(2,1)S(1)}, u32[]{:S(2)}, u32[]{:S(2)}) async-start(bf16[16,36,1024]{2,1,0:T(8,128)(2,1)} %reshape_reshape.14), calls=%async_computation.2 | async-start | bytes 2621440 | tf_op jit(solution)/shard_map/all_to_all | solution.py:106
  47.9 11.5 %slice-start = ((s8[8388608]{0:T(1024)(128)(4,1)}), s8[4194304]{0:T(1024)(128)(4,1)S(1)}, s32[]{:S(2)}) async-start(s8[8388608]{0:T(1024)(128)(4,1)} %bitcast.75), calls=%async_computation.4 | async-start | bytes 8388608
  48.6 10.8 %copy-start.3 = (bf16[16,36,1024]{2,0,1:T(8,128)(2,1)}, bf16[16,36,1024]{2,0,1:T(8,128)(2,1)S(1)}, u32[]{:S(2)}) copy-start(bf16[16,36,1024]{2,0,1:T(8,128)(2,1)S(1)} %copy.43) | copy-start | bytes 3538948
  48.6 10.8 %slice-start.1 = ((s8[8388608]{0:T(1024)(128)(4,1)}), s8[4194304]{0:T(1024)(128)(4,1)S(1)}, s32[]{:S(2)}) async-start(s8[8388608]{0:T(1024)(128)(4,1)} %bitcast.75), calls=%async_computation.5 | async-start | bytes 8388608
  59.4 3.7 %copy-start.8 = (f32[2,16,18,2048]{3,2,1,0:T(8,128)}, f32[2,16,18,2048]{3,2,1,0:T(8,128)S(1)}, u32[]{:S(2)}) copy-start(f32[2,16,18,2048]{3,2,1,0:T(8,128)S(1)} %fusion.2) | copy-start | bytes 14155780
  78.3 1.1 copy-start.2
  79.4 63.6 %all-to-all-start.1 = ((f32[16,36,1024]{2,1,0:T(8,128)}), f32[16,36,1024]{2,1,0:T(8,128)S(1)}, u32[]{:S(2)}, u32[]{:S(2)}) async-start(f32[16,36,1024]{2,1,0:T(8,128)} %copy.47), calls=%async_computation.1 | async-start | bytes 5242880 | tf_op jit(solution)/shard_map/all_to_all | solution.py:105
  86.4 11.9 %copy-start.4 = (bf16[16,36,1024]{2,0,1:T(8,128)(2,1)}, bf16[16,36,1024]{2,0,1:T(8,128)(2,1)S(1)}, u32[]{:S(2)}) copy-start(bf16[16,36,1024]{2,0,1:T(8,128)(2,1)S(1)} %copy.49) | copy-start | bytes 3538948
  98.3 13.0 %copy-start.9 = (bf16[16,2,18,2048]{3,2,0,1:T(8,128)(2,1)}, bf16[16,2,18,2048]{3,2,0,1:T(8,128)(2,1)S(1)}, u32[]{:S(2)}) copy-start(bf16[16,2,18,2048]{3,2,0,1:T(8,128)(2,1)S(1)} %fusion.5) | copy-start | bytes 7077892
  143.0 63.8 %all-to-all-start.3 = ((f32[16,36,1024]{2,1,0:T(8,128)}), f32[16,36,1024]{2,1,0:T(8,128)}, u32[]{:S(2)}, u32[]{:S(2)}) async-start(f32[16,36,1024]{2,1,0:T(8,128)} %copy.53), calls=%async_computation.3 | async-start | bytes 5242880 | tf_op jit(solution)/shard_map/all_to_all | solution.py:110
  184.3 26.3 %copy-start.1 = (bf16[128,1024]{1,0:T(8,128)(2,1)S(1)}, bf16[128,1024]{1,0:T(8,128)(2,1)}, u32[]{:S(2)}) copy-start(bf16[128,1024]{1,0:T(8,128)(2,1)} %param.7) | copy-start | bytes 786436
where the time goes:
time: 215 us; the launch traced here: 211 us
  waiting for transfers between devices  70.9 us (33%)
  matrix products  68.8 us (32%)
  local copies, waits for them, and re-layouts  45 us (21%)
  starting transfers between devices  21.7 us (10%)
  other arithmetic  3.32 us (2%)
    all_to_all x1, waiting for transfers between devices, per_device(): lax.all_to_all(outputs, 'expert', split_axis=0, concat_axis=0, tiled=True)  27.4 us
    all_to_all x1, waiting for transfers between devices, per_device(): lax.all_to_all(partial_grads, 'expert', split_axis=0, concat_axis=0, tile...  18.7 us
    reshape x1, local copies, waits for them, and re-layouts, per_device(): up_local = up_proj.reshape(hidden_width, local_count, local_units)  14.5 us
    all_to_all x1, waiting for transfers between devices, per_device(): lax.all_to_all(sent_rows, 'expert', split_axis=0, concat_axis=0, tiled=True)  13.8 us
    unnamed x26, local copies, waits for them, and re-layouts  13.1 us
    dot_general x1, matrix products, backward_part(): jnp.einsum('nlcf,dlf->nlcd', pre_grad, up_local, preferred_element_type=j...  13 us
    dot_general x1, matrix products, backward_part(): jnp.einsum('nlcf,nlcd->lfd', act, scaled, preferred_element_type=jnp.floa...  12.1 us
    dot_general x1, matrix products, backward_part(): jnp.einsum('nlcd,lfd->nlcf', scaled, down_local, preferred_element_type=j...  11.9 us
  transfers between devices with their start and end apart: 4, of which 4 were waited for; matrix products, arithmetic and copies ran while one was open for 51% of the time, Pallas kernels for 0%

commit v1 on v0

--- a/solution.py
+++ b/solution.py
@@ -1,6 +1,10 @@
+import functools
+
 import jax
 import jax.numpy as jnp
 from jax import lax
+from jax.experimental import pallas as pl
+from jax.experimental.pallas import tpu as pltpu
 from jax.sharding import PartitionSpec as P
 
 FF = 2048
@@ -8,6 +12,9 @@
 TASKS = 8
 K = 4
 CAP = 18
+PLANE = 4
+SPAN = 256
+TILE = 512
 
 
 def block_route(counts, expert_list, mix_flat, row_total):
@@ -76,7 +83,7 @@
     )
 
 
-def per_device(rows, cotangent, up_proj, down_proj, mix_weight, task_counts, expert_order):
+def direct_plan(rows, cotangent, up_proj, down_proj, mix_weight, task_counts, expert_order):
     owners = lax.axis_size("expert")
     row_total = rows.shape[0]
     hidden_width = rows.shape[1]
@@ -120,6 +127,362 @@
         jnp.bfloat16
     )
     return (mixed, row_gradient, up_grad, down_grad)
+
+
+def grad_kernel(a_ref, b_ref, o_ref):
+    o_ref[...] = lax.dot_general(
+        a_ref[0], b_ref[0], (((0,), (0,)), ((), ())), preferred_element_type=jnp.float32
+    ).astype(o_ref.dtype)
+
+
+def cost(local_count, slots, units, width):
+    return pl.CostEstimate(
+        flops=2 * local_count * slots * units * width,
+        bytes_accessed=2 * local_count * (units * width + slots * (units + width)),
+        transcendentals=0,
+    )
+
+
+def up_grad_call(inputs, pre_grad):
+    local_count, slots, width = inputs.shape
+    units = pre_grad.shape[2]
+    tile = min(512, units)
+    return pl.pallas_call(
+        grad_kernel,
+        grid=(local_count, units // tile),
+        in_specs=[
+            pl.BlockSpec((1, slots, width), lambda l, j: (l, 0, 0)),
+            pl.BlockSpec((1, slots, tile), lambda l, j: (l, 0, j)),
+        ],
+        out_specs=pl.BlockSpec((width, tile), lambda l, j: (0, l * (units // tile) + j)),
+        out_shape=jax.ShapeDtypeStruct((width, local_count * units), jnp.bfloat16),
+        cost_estimate=cost(local_count, slots, units, width),
+    )(inputs, pre_grad)
+
+
+def down_grad_call(act, scaled):
+    local_count, slots, width = scaled.shape
+    units = act.shape[2]
+    tile = min(512, units)
+    return pl.pallas_call(
+        grad_kernel,
+        grid=(local_count, units // tile),
+        in_specs=[
+            pl.BlockSpec((1, slots, tile), lambda l, j: (l, 0, j)),
+            pl.BlockSpec((1, slots, width), lambda l, j: (l, 0, 0)),
+        ],
+        out_specs=pl.BlockSpec((tile, width), lambda l, j: (l * (units // tile) + j, 0)),
+        out_shape=jax.ShapeDtypeStruct((local_count * units, width), jnp.bfloat16),
+        cost_estimate=cost(local_count, slots, units, width),
+    )(act, scaled)
+
+
+def dot_nt(a, b):
+    return lax.dot_general(a, b, (((1,), (1,)), ((), ())), preferred_element_type=jnp.float32)
+
+
+def dot_tn(a, b):
+    return lax.dot_general(a, b, (((0,), (0,)), ((), ())), preferred_element_type=jnp.float32)
+
+
+def slot_places(counts, order, mix_flat, me, line, local_count, pad, row_total, width):
+    firsts = jnp.cumsum(counts) - counts
+    matches = order[None, :] == jnp.arange(EXPERTS, dtype=jnp.int32)[:, None]
+    count_of = jnp.sum(jnp.where(matches, jnp.repeat(counts, K)[None], 0), axis=1)
+    first_of = jnp.sum(jnp.where(matches, jnp.repeat(firsts, K)[None], 0), axis=1)
+    weight_of = jnp.sum(jnp.where(matches, mix_flat[None], 0.0), axis=1)
+    lane = jnp.arange(width, dtype=jnp.int32)
+    member, inner = lane // SPAN, lane % SPAN
+    local, spot = inner // pad, inner % pad
+    slot = spot - (me // PLANE) * CAP
+    known = (member < PLANE) & (local < local_count) & (slot >= 0) & (slot < CAP)
+    expert = (jnp.arange(line)[:, None] * PLANE + member[None]) * local_count + local[None]
+    here = expert[:, :, None] == jnp.arange(EXPERTS, dtype=jnp.int32)
+    spread = lambda v: jnp.sum(jnp.where(here, v[None, None], 0), axis=-1)
+    filled = known[None] & (slot[None] < spread(count_of))
+    target = jnp.where(filled, spread(first_of) + slot[None], -1).astype(jnp.float32)
+    weight = jnp.where(filled, spread(weight_of), 0.0)
+    high = lax.reduce_precision(weight, 8, 7)
+    middle = lax.reduce_precision(weight - high, 8, 7)
+    low = weight - high - middle
+    return jnp.concatenate([target, high, middle, low]).astype(jnp.bfloat16)
+
+
+def plane_kernel(
+    line, local_count, pad,
+    rows_ref, cot_ref, up_hbm, down_hbm,
+    mixed_ref, part_ref, x_ref, s_ref, act_ref, pg_ref,
+    rows_all, cot_all, up_ref, down_ref, sel, whi, wmid, wlo,
+    x_send, s_send, o_send, d_send, o_got, d_got, pre_ref, acc_ref, m_send, m_got,
+    w_sem, l_sem, r_ss, r_rs, c_ss, c_rs, x_ss, x_rs, s_ss, s_rs, o_ss, o_rs, d_ss, d_rs, m_ss, m_rs,
+):
+    me = lax.axis_index("expert")
+    z, p = me // PLANE, lax.rem(me, PLANE)
+    row_total, width = cot_ref.shape
+    f32, bf16 = jnp.float32, jnp.bfloat16
+
+    weights_in = [
+        pltpu.make_async_copy(up_hbm, up_ref, w_sem.at[0]),
+        pltpu.make_async_copy(down_hbm, down_ref, w_sem.at[1]),
+    ]
+    own = [
+        pltpu.make_async_copy(rows_ref, rows_all.at[z], l_sem.at[0]),
+        pltpu.make_async_copy(cot_ref, cot_all.at[z], l_sem.at[1]),
+    ]
+    for copy in own:
+        copy.start()
+    barrier = pltpu.get_barrier_semaphore()
+    for k in range(1, PLANE):
+        pl.semaphore_signal(barrier, inc=1, device_id={"expert": z * PLANE + lax.rem(p + k, PLANE)})
+    for k in range(1, line):
+        pl.semaphore_signal(barrier, inc=1, device_id={"expert": lax.rem(z + k, line) * PLANE + p})
+    pl.semaphore_wait(barrier, PLANE - 1 + line - 1)
+    for copy in own:
+        copy.wait()
+    for copy in weights_in:
+        copy.start()
+
+    def hop(buf, j, shift, ss, rs, lane):
+        return pltpu.make_async_remote_copy(
+            src_ref=buf.at[j], dst_ref=buf.at[j],
+            send_sem=ss.at[lane, j], recv_sem=rs.at[j],
+            device_id={"expert": lax.rem(me + (line + shift) * PLANE, line * PLANE)},
+        )
+
+    def pass_on(buf, j, shift, ss, rs):
+        @pl.when((z + shift >= 0) & (z + shift < line))
+        def _():
+            hop(buf, j, shift, ss, rs, 0 if shift == 1 else 1).start()
+
+    def settle(buf, ss, rs):
+        for d in range(line):
+            for shift in (1, -1):
+                j = z - shift * d
+                @pl.when((j >= 0) & (j < line) & (z + shift >= 0) & (z + shift < line))
+                def _():
+                    hop(buf, j, shift, ss, rs, 0 if shift == 1 else 1).wait_send()
+
+    def gather_step(buf, d, ss, rs, after=None):
+        for shift in (1, -1):
+            j = z - shift * d
+            @pl.when((j >= 0) & (j < line))
+            def _():
+                if d > 0:
+                    hop(buf, j, shift, ss, rs, 0).wait_recv()
+                pass_on(buf, j, shift, ss, rs)
+            if after is not None:
+                @pl.when(j == (0 if shift == 1 else line - 1))
+                def _():
+                    pass_on(after[0], z, shift, after[1], after[2])
+
+    for d in range(line):
+        gather_step(rows_all, d, r_ss, r_rs, (cot_all, c_ss, c_rs))
+
+    for j in range(line):
+        info = rows_all[j, row_total:, :].astype(f32)
+        at = lax.broadcasted_iota(jnp.int32, info.shape, 0)
+        pick = lambda q: jnp.sum(jnp.where(at == q * line + z, info, 0.0), axis=0, keepdims=True)
+        hit = lax.broadcasted_iota(jnp.int32, (row_total, width), 0) == pick(0).astype(jnp.int32)
+        block = pl.ds(j * row_total, row_total)
+        sel[block, :] = jnp.where(hit, 1.0, 0.0).astype(bf16)
+        for ref, q in ((whi, 1), (wmid, 2), (wlo, 3)):
+            ref[block, :] = jnp.where(hit, pick(q), 0.0).astype(bf16)
+
+    def swap(send, got, ss, rs, l, k):
+        to = lax.rem(p + k, PLANE)
+        return pltpu.make_async_remote_copy(
+            src_ref=send.at[l, pl.ds(pl.multiple_of(to * pad, 16), pad)],
+            dst_ref=got.at[l, pl.ds(pl.multiple_of(p * pad, 16), pad)],
+            send_sem=ss.at[l, k], recv_sem=rs.at[l, k],
+            device_id={"expert": z * PLANE + to},
+        )
+
+    def keep(send, got, rs, l):
+        place = pl.ds(pl.multiple_of(p * pad, 16), pad)
+        return pltpu.make_async_copy(send.at[l, place], got.at[l, place], rs.at[l, 0])
+
+    def swap_start(send, got, ss, rs, l):
+        for k in range(1, PLANE):
+            swap(send, got, ss, rs, l, k).start()
+        keep(send, got, rs, l).start()
+
+    def swap_wait(send, got, ss, rs, l):
+        for k in range(1, PLANE):
+            swap(send, got, ss, rs, l, k).wait()
+        keep(send, got, rs, l).wait()
+
+    def dispatch(values, refs, send, got, ss, rs):
+        for q in range(PLANE):
+            lanes = pl.ds(q * SPAN, SPAN)
+            picked = sum(dot_tn(ref[:, lanes], values) for ref in refs).astype(bf16)
+            for l in range(local_count):
+                send[l, q * pad : (q + 1) * pad, :] = picked[l * pad : (l + 1) * pad]
+        for l in range(local_count):
+            swap_start(send, got, ss, rs, l)
+
+    dispatch(
+        rows_all[:, :row_total, :].reshape(line * row_total, width), [sel], x_send, x_ref, x_ss, x_rs
+    )
+    for d in range(1, line):
+        gather_step(cot_all, d, c_ss, c_rs)
+    dispatch(
+        cot_all[...].reshape(line * row_total, width), [whi, wmid, wlo], s_send, s_ref, s_ss, s_rs
+    )
+    for copy in weights_in:
+        copy.wait()
+
+    for l in range(local_count):
+        swap_wait(x_send, x_ref, x_ss, x_rs, l)
+        acc_ref[...] = jnp.zeros_like(acc_ref)
+
+        @pl.loop(0, FF // TILE)
+        def _(f):
+            own_units = pl.ds(pl.multiple_of(f * TILE, TILE), TILE)
+            units = pl.ds(pl.multiple_of(l * FF + f * TILE, TILE), TILE)
+            pre = jnp.dot(x_ref[l], up_ref[:, units], preferred_element_type=f32)
+            act = (pre / (1.0 + jnp.exp(-pre))).astype(bf16)
+            pre_ref[l, :, own_units] = pre
+            act_ref[l, :, own_units] = act
+            acc_ref[...] += jnp.dot(act, down_ref[units, :], preferred_element_type=f32)
+
+        o_send[l] = acc_ref[...].astype(bf16)
+        swap_start(o_send, o_got, o_ss, o_rs, l)
+
+    def back(l):
+        swap_wait(s_send, s_ref, s_ss, s_rs, l)
+        acc_ref[...] = jnp.zeros_like(acc_ref)
+
+        @pl.loop(0, FF // TILE)
+        def _(f):
+            own_units = pl.ds(pl.multiple_of(f * TILE, TILE), TILE)
+            units = pl.ds(pl.multiple_of(l * FF + f * TILE, TILE), TILE)
+            act_grad = dot_nt(s_ref[l], down_ref[units, :])
+            pre = pre_ref[l, :, own_units]
+            sg = 1.0 / (1.0 + jnp.exp(-pre))
+            pre_grad = (act_grad * sg * (1.0 + pre * (1.0 - sg))).astype(bf16)
+            pg_ref[l, :, own_units] = pre_grad
+            acc_ref[...] += dot_nt(pre_grad, up_ref[:, units])
+
+        d_send[l] = acc_ref[...].astype(bf16)
+        swap_start(d_send, d_got, d_ss, d_rs, l)
+
+    def combined(got, refs, j):
+        block = pl.ds(j * row_total, row_total)
+        total = jnp.zeros((row_total, width), f32)
+        for q in range(PLANE):
+            slots = jnp.concatenate(
+                [got[l, q * pad : (q + 1) * pad, :] for l in range(local_count)]
+                + [jnp.zeros((SPAN - local_count * pad, width), bf16)],
+                axis=0,
+            )
+            for ref in refs:
+                total += jnp.dot(ref[block, pl.ds(q * SPAN, SPAN)], slots, preferred_element_type=f32)
+        return total
+
+    def home(k):
+        to = lax.rem(z + k, line)
+        return pltpu.make_async_remote_copy(
+            src_ref=m_send.at[to], dst_ref=m_got.at[z],
+            send_sem=m_ss.at[k], recv_sem=m_rs.at[k],
+            device_id={"expert": to * PLANE + p},
+        )
+
+    back(0)
+    for l in range(local_count):
+        swap_wait(o_send, o_got, o_ss, o_rs, l)
+    for j in range(line):
+        m_send[j] = combined(o_got, [whi, wmid], j).astype(bf16)
+    for k in range(1, line):
+        home(k).start()
+    keep_mixed = pltpu.make_async_copy(m_send.at[z], m_got.at[z], m_rs.at[0])
+    keep_mixed.start()
+    for l in range(1, local_count):
+        back(l)
+    for l in range(local_count):
+        swap_wait(d_send, d_got, d_ss, d_rs, l)
+    for j in range(line):
+        part_ref[j] = combined(d_got, [sel], j).astype(bf16)
+    for k in range(1, line):
+        home(k).wait()
+    keep_mixed.wait()
+    mixed_ref[...] = sum(m_got[j].astype(f32) for j in range(line)).astype(bf16)
+    settle(rows_all, r_ss, r_rs)
+    settle(cot_all, c_ss, c_rs)
+
+
+def plane_call(rows, cotangent, up_proj, down_proj, line, local_count, pad):
+    bf16, f32 = jnp.bfloat16, jnp.float32
+    row_total, width = cotangent.shape
+    taken = PLANE * pad
+    slots = (local_count, taken, width)
+    wide = (local_count, taken, FF)
+    dma = pltpu.SemaphoreType.DMA
+    vmem, anywhere = pl.BlockSpec(memory_space=pltpu.VMEM), pl.BlockSpec(memory_space=pl.ANY)
+    table = pltpu.VMEM((line * row_total, width), bf16)
+    blocks = (line, row_total, width)
+    swaps = (local_count, PLANE)
+    return pl.pallas_call(
+        functools.partial(plane_kernel, line, local_count, pad),
+        out_shape=[
+            jax.ShapeDtypeStruct((row_total, width), bf16),
+            jax.ShapeDtypeStruct(blocks, bf16),
+            jax.ShapeDtypeStruct(slots, bf16),
+            jax.ShapeDtypeStruct(slots, bf16),
+            jax.ShapeDtypeStruct(wide, bf16),
+            jax.ShapeDtypeStruct(wide, bf16),
+        ],
+        in_specs=[vmem, vmem, anywhere, anywhere],
+        out_specs=[vmem] * 6,
+        scratch_shapes=[
+            pltpu.VMEM((line,) + rows.shape, bf16),
+            pltpu.VMEM(blocks, bf16),
+            pltpu.VMEM(up_proj.shape, bf16),
+            pltpu.VMEM(down_proj.shape, bf16),
+        ]
+        + [table] * 4
+        + [pltpu.VMEM(slots, bf16)] * 6
+        + [pltpu.VMEM(wide, f32), pltpu.VMEM((taken, width), f32)]
+        + [pltpu.VMEM(blocks, bf16)] * 2
+        + [dma((2,)), dma((2,))]
+        + [dma((2, line)), dma((line,))] * 2
+        + [dma(swaps)] * 8
+        + [dma((line,))] * 2,
+        compiler_params=pltpu.CompilerParams(
+            collective_id=0, has_side_effects=True, vmem_limit_bytes=60 << 20
+        ),
+    )(rows, cotangent, up_proj, down_proj)
+
+
+def plane_plan(rows, cotangent, up_proj, down_proj, mix_weight, task_counts, expert_order):
+    owners = lax.axis_size("expert")
+    me = lax.axis_index("expert")
+    line = owners // PLANE
+    row_total, width = rows.shape
+    local_count = up_proj.shape[1] // FF
+    pad = (line * CAP + 15) // 16 * 16
+    places = slot_places(
+        task_counts[0], expert_order[0], mix_weight.reshape(-1),
+        me, line, local_count, pad, row_total, width,
+    )
+    mixed, parts, inputs, scaled, act, pre_grad = plane_call(
+        jnp.concatenate([rows, places]), cotangent, up_proj, down_proj, line, local_count, pad
+    )
+    groups = [[z * PLANE + p for z in range(line)] for p in range(PLANE)]
+    home = lax.all_to_all(parts, "expert", 0, 0, axis_index_groups=groups, tiled=True)
+    up_grad = up_grad_call(inputs, pre_grad)
+    down_grad = down_grad_call(act, scaled)
+    row_gradient = jnp.sum(home.astype(jnp.float32), axis=0).astype(jnp.bfloat16)
+    return (mixed, row_gradient, up_grad, down_grad)
+
+
+def per_device(rows, cotangent, up_proj, *others):
+    owners = lax.axis_size("expert")
+    whole_experts = up_proj.shape[1] % FF == 0
+    local_count = up_proj.shape[1] // FF
+    fits = owners % PLANE == 0 and local_count * (-(-owners // PLANE * CAP // 16) * 16) <= SPAN
+    wide_plane = fits and owners > PLANE and rows.shape[1] == PLANE * SPAN
+    plan = plane_plan if whole_experts and wide_plane else direct_plan
+    return plan(rows, cotangent, up_proj, *others)
 
 
 def solution(mesh):

time: 215 us -> 144 us (0.67)
  the two profiles are of different devices: /device:TPU:15 before, /device:TPU:0 now
where the time goes in v1:
time: 144 us
  Pallas kernels  122 us (85%)
  waiting for transfers between devices  5.83 us (4%)
  starting transfers between devices  5.56 us (4%)
  local copies, waits for them, and re-layouts  5.41 us (4%)
  other arithmetic  4.51 us (3%)
    pallas_call x1, Pallas kernels, plane_call(): pl.pallas_call(functools.partial(plane_kernel, line, local_count, pad), o...  101 us
    pallas_call x1, Pallas kernels, down_grad_call(): pl.pallas_call(grad_kernel, grid=(local_count, units // tile), in_specs=[...  10.2 us
    pallas_call x1, Pallas kernels, up_grad_call(): pl.pallas_call(grad_kernel, grid=(local_count, units // tile), in_specs=[...  10.1 us
    all_to_all x1, waiting for transfers between devices, plane_plan(): lax.all_to_all(parts, 'expert', 0, 0, axis_index_groups=groups, tiled=True)  5.83 us
    all_to_all x1, starting transfers between devices, plane_plan(): lax.all_to_all(parts, 'expert', 0, 0, axis_index_groups=groups, tiled=True)  5.56 us
    concatenate x1, local copies, waits for them, and re-layouts, plane_plan(): jnp.concatenate([rows, places])  2.9 us
  transfers between devices with their start and end apart: 1, of which 1 were waited for; matrix products, arithmetic and copies ran while one was open for 0% of the time, Pallas kernels for 14%

profile of v1, /device:TPU:0, one launch (start us, length us, event | category | flops | bytes accessed | tf_op | source)
XLA Modules:
  0.0 143.6 jit_solution(7520901187440202093)
XLA Ops:
  0.7 0.8 reduce-window.9
  1.6 0.7 bitcast_subtract_fusion
  2.2 0.1 broadcast_in_dim.98
  2.3 0.1 broadcast_in_dim.99
  2.4 0.8 copy.13
  3.1 0.1 broadcast_in_dim.103
  3.2 0.7 broadcast_in_dim.92
  3.9 0.1 broadcast_in_dim.93
  4.0 0.8 select_reduce_fusion.3
  4.8 0.8 select_reduce_fusion.4
  5.6 0.1 multiply_add_fusion
  5.6 0.2 select_reduce_fusion
  5.8 0.2 select_reduce_fusion.1
  6.1 2.9 %concatenate.6.rows_ref = bf16[144,1024]{1,0:T(8,128)(2,1)} concatenate(bf16[128,1024]{1,0:T(8,128)(2,1)} %param.7, bf16[4,1024]{1,0:T(4,128)(2,1)S(1)} %convert_convert_fusion, bf16[4,1024]{1,0:T(4,128)(2,1)S(1)} %get-tuple-element.23, bf16[4,1024]{1,0:T(4,128)(2,1)S(1)} %get-tuple-element.22, bf16[4,1024]{1,0:T(4,128)(2,1)S(1)} %get-tuple-element.20), dimensions={0} | concatenate | bytes 589824 | tf_op jit(solution)/shard_map/concatenate | solution.py:468
  9.0 101.3 %shard_map.102 = (bf16[128,1024]{1,0:T(8,128)(2,1)}, bf16[4,128,1024]{2,1,0:T(8,128)(2,1)}, bf16[2,320,1024]{2,1,0:T(8,128)(2,1)}, bf16[2,320,1024]{2,1,0:T(8,12...) custom-call(bf16[144,1024]{1,0:T(8,128)(2,1)} %concatenate.6.rows_ref, bf16[128,1024]{1,0:T(8,128)(2,1)} %cot_ref.1, ...), custom_call_target="tpu_custom_call" | custom-call | tf_op jit(solution)/shard_map/pallas_call | solution.py:424
  110.3 5.6 %all-to-all-start = ((bf16[4,128,1024]{2,1,0:T(8,128)(2,1)}), bf16[4,128,1024]{2,1,0:T(8,128)(2,1)S(1)}, u32[]{:S(2)}, u32[]{:S(2)}) async-start(bf16[4,128,1024]{2,1,0:T(8,128)(2,1)} %get-tuple-element.11), calls=%async_computation | async-start | bytes 2097152 | tf_op jit(solution)/shard_map/all_to_all | solution.py:471
  115.8 10.1 %shard_map.103 = bf16[1024,4096]{1,0:T(8,128)(2,1)} custom-call(bf16[2,320,1024]{2,1,0:T(8,128)(2,1)} %get-tuple-element.12.a_ref, bf16[2,320,2048]{2,1,0:T(8,128)(2,1)} %get-tuple-element.13.b_ref), custom_call_target="tpu_custom_call" | custom-call | flops 2684354560 | bytes 12320768 | tf_op jit(solution)/shard_map/pallas_call | solution.py:150
  126.0 0.0 copy-start
  126.0 10.2 %shard_map.104 = bf16[4096,1024]{1,0:T(8,128)(2,1)} custom-call(bf16[2,320,2048]{2,1,0:T(8,128)(2,1)} %get-tuple-element.14.a_ref, bf16[2,320,1024]{2,1,0:T(8,128)(2,1)} %get-tuple-element.15.b_ref), custom_call_target="tpu_custom_call" | custom-call | flops 2684354560 | bytes 12320768 | tf_op jit(solution)/shard_map/pallas_call | solution.py:167
  136.1 5.8 %all-to-all-done = bf16[4,128,1024]{2,1,0:T(8,128)(2,1)S(1)} async-done(((bf16[4,128,1024]{2,1,0:T(8,128)(2,1)}), bf16[4,128,1024]{2,1,0:T(8,128)(2,1)S(1)}, u32[]{:S(2)}, u32[]{:S(2)}) %all-to-all-start) | async-done | bytes 1048608 | tf_op jit(solution)/shard_map/all_to_all | solution.py:471
  142.0 0.9 reduce_sum.72
  142.9 0.0 copy-done
  142.9 0.7 copy.15
  (7 shorter events, 0.1 us)
Async XLA Ops:
  110.3 31.7 %all-to-all-start = ((bf16[4,128,1024]{2,1,0:T(8,128)(2,1)}), bf16[4,128,1024]{2,1,0:T(8,128)(2,1)S(1)}, u32[]{:S(2)}, u32[]{:S(2)}) async-start(bf16[4,128,1024]{2,1,0:T(8,128)(2,1)} %get-tuple-element.11), calls=%async_computation | async-start | bytes 2097152 | tf_op jit(solution)/shard_map/all_to_all | solution.py:471
  126.0 16.9 %copy-start = (bf16[128,1024]{1,0:T(8,128)(2,1)S(1)}, bf16[128,1024]{1,0:T(8,128)(2,1)}, u32[]{:S(2)}) copy-start(bf16[128,1024]{1,0:T(8,128)(2,1)} %get-tuple-element.30) | copy-start | bytes 786436

commit v2 on v1

--- a/solution.py
+++ b/solution.py
@@ -13,7 +13,6 @@
 K = 4
 CAP = 18
 PLANE = 4
-SPAN = 256
 TILE = 512
 
 
@@ -186,16 +185,16 @@
 
 
 def slot_places(counts, order, mix_flat, me, line, local_count, pad, row_total, width):
-    firsts = jnp.cumsum(counts) - counts
+    task = jnp.arange(TASKS)
+    firsts = jnp.sum(jnp.where(task[None, :] < task[:, None], counts[None, :], 0), axis=1)
     matches = order[None, :] == jnp.arange(EXPERTS, dtype=jnp.int32)[:, None]
     count_of = jnp.sum(jnp.where(matches, jnp.repeat(counts, K)[None], 0), axis=1)
     first_of = jnp.sum(jnp.where(matches, jnp.repeat(firsts, K)[None], 0), axis=1)
     weight_of = jnp.sum(jnp.where(matches, mix_flat[None], 0.0), axis=1)
     lane = jnp.arange(width, dtype=jnp.int32)
-    member, inner = lane // SPAN, lane % SPAN
-    local, spot = inner // pad, inner % pad
+    member, local, spot = lane // pad % PLANE, lane // pad // PLANE, lane % pad
     slot = spot - (me // PLANE) * CAP
-    known = (member < PLANE) & (local < local_count) & (slot >= 0) & (slot < CAP)
+    known = (local < local_count) & (slot >= 0) & (slot < CAP)
     expert = (jnp.arange(line)[:, None] * PLANE + member[None]) * local_count + local[None]
     here = expert[:, :, None] == jnp.arange(EXPERTS, dtype=jnp.int32)
     spread = lambda v: jnp.sum(jnp.where(here, v[None, None], 0), axis=-1)
@@ -210,11 +209,11 @@
 
 def plane_kernel(
     line, local_count, pad,
-    rows_ref, cot_ref, up_hbm, down_hbm,
-    mixed_ref, part_ref, x_ref, s_ref, act_ref, pg_ref,
-    rows_all, cot_all, up_ref, down_ref, sel, whi, wmid, wlo,
+    rows_ref, places_ref, cot_ref, up_hbm, down_hbm,
+    mixed_ref, part_ref, x_out, s_out, act_out, pg_out,
+    rows_all, cot_all, up_ref, down_ref, sel, w_ref, x_ref, s_ref, act_ref, pg_ref,
     x_send, s_send, o_send, d_send, o_got, d_got, pre_ref, acc_ref, m_send, m_got,
-    w_sem, l_sem, r_ss, r_rs, c_ss, c_rs, x_ss, x_rs, s_ss, s_rs, o_ss, o_rs, d_ss, d_rs, m_ss, m_rs,
+    w_sem, l_sem, out_sem, r_ss, r_rs, c_ss, c_rs, x_ss, x_rs, s_ss, s_rs, o_ss, o_rs, d_ss, d_rs, m_ss, m_rs,
 ):
     me = lax.axis_index("expert")
     z, p = me // PLANE, lax.rem(me, PLANE)
@@ -226,8 +225,11 @@
         pltpu.make_async_copy(down_hbm, down_ref, w_sem.at[1]),
     ]
     own = [
-        pltpu.make_async_copy(rows_ref, rows_all.at[z], l_sem.at[0]),
+        pltpu.make_async_copy(rows_ref, rows_all.at[z, pl.ds(0, row_total)], l_sem.at[0]),
         pltpu.make_async_copy(cot_ref, cot_all.at[z], l_sem.at[1]),
+        pltpu.make_async_copy(
+            places_ref, rows_all.at[z, pl.ds(row_total, places_ref.shape[0])], l_sem.at[2]
+        ),
     ]
     for copy in own:
         copy.start()
@@ -278,15 +280,16 @@
     for d in range(line):
         gather_step(rows_all, d, r_ss, r_rs, (cot_all, c_ss, c_rs))
 
+    lanes = sel.shape[1]
+    weight = jnp.zeros((1, lanes), f32)
     for j in range(line):
-        info = rows_all[j, row_total:, :].astype(f32)
+        info = rows_all[j, row_total:, :lanes].astype(f32)
         at = lax.broadcasted_iota(jnp.int32, info.shape, 0)
         pick = lambda q: jnp.sum(jnp.where(at == q * line + z, info, 0.0), axis=0, keepdims=True)
-        hit = lax.broadcasted_iota(jnp.int32, (row_total, width), 0) == pick(0).astype(jnp.int32)
-        block = pl.ds(j * row_total, row_total)
-        sel[block, :] = jnp.where(hit, 1.0, 0.0).astype(bf16)
-        for ref, q in ((whi, 1), (wmid, 2), (wlo, 3)):
-            ref[block, :] = jnp.where(hit, pick(q), 0.0).astype(bf16)
+        hit = lax.broadcasted_iota(jnp.int32, (row_total, lanes), 0) == pick(0).astype(jnp.int32)
+        sel[j * row_total : (j + 1) * row_total, :] = jnp.where(hit, 1.0, 0.0).astype(bf16)
+        weight += pick(1) + pick(2) + pick(3)
+    w_ref[...] = jnp.transpose(jnp.broadcast_to(weight, (w_ref.shape[1], lanes)))
 
     def swap(send, got, ss, rs, l, k):
         to = lax.rem(p + k, PLANE)
@@ -311,28 +314,24 @@
             swap(send, got, ss, rs, l, k).wait()
         keep(send, got, rs, l).wait()
 
-    def dispatch(values, refs, send, got, ss, rs):
-        for q in range(PLANE):
-            lanes = pl.ds(q * SPAN, SPAN)
-            picked = sum(dot_tn(ref[:, lanes], values) for ref in refs).astype(bf16)
-            for l in range(local_count):
-                send[l, q * pad : (q + 1) * pad, :] = picked[l * pad : (l + 1) * pad]
+    taken = PLANE * pad
+
+    def leave(ref, out, n, l):
+        return pltpu.make_async_copy(ref.at[l], out.at[l], out_sem.at[n, l])
+
+    def dispatch(values, scale, send, got, ss, rs):
+        picked = dot_tn(sel[...], values)
+        if scale is not None:
+            picked = scale * picked
+        picked = picked.astype(bf16)
+        for l in range(local_count):
+            send[l] = picked[l * taken : (l + 1) * taken]
         for l in range(local_count):
             swap_start(send, got, ss, rs, l)
 
-    dispatch(
-        rows_all[:, :row_total, :].reshape(line * row_total, width), [sel], x_send, x_ref, x_ss, x_rs
-    )
-    for d in range(1, line):
-        gather_step(cot_all, d, c_ss, c_rs)
-    dispatch(
-        cot_all[...].reshape(line * row_total, width), [whi, wmid, wlo], s_send, s_ref, s_ss, s_rs
-    )
-    for copy in weights_in:
-        copy.wait()
-
-    for l in range(local_count):
+    def forward(l):
         swap_wait(x_send, x_ref, x_ss, x_rs, l)
+        leave(x_ref, x_out, 0, l).start()
         acc_ref[...] = jnp.zeros_like(acc_ref)
 
         @pl.loop(0, FF // TILE)
@@ -347,9 +346,26 @@
 
         o_send[l] = acc_ref[...].astype(bf16)
         swap_start(o_send, o_got, o_ss, o_rs, l)
+        leave(act_ref, act_out, 2, l).start()
+
+    dispatch(
+        rows_all[:, :row_total, :].reshape(line * row_total, width), None, x_send, x_ref, x_ss, x_rs
+    )
+    for d in range(1, line - 1):
+        gather_step(cot_all, d, c_ss, c_rs)
+    for copy in weights_in:
+        copy.wait()
+    forward(0)
+    gather_step(cot_all, line - 1, c_ss, c_rs)
+    dispatch(
+        cot_all[...].reshape(line * row_total, width), w_ref[:, :1], s_send, s_ref, s_ss, s_rs
+    )
+    for l in range(1, local_count):
+        forward(l)
 
     def back(l):
         swap_wait(s_send, s_ref, s_ss, s_rs, l)
+        leave(s_ref, s_out, 1, l).start()
         acc_ref[...] = jnp.zeros_like(acc_ref)
 
         @pl.loop(0, FF // TILE)
@@ -365,19 +381,11 @@
 
         d_send[l] = acc_ref[...].astype(bf16)
         swap_start(d_send, d_got, d_ss, d_rs, l)
-
-    def combined(got, refs, j):
-        block = pl.ds(j * row_total, row_total)
-        total = jnp.zeros((row_total, width), f32)
-        for q in range(PLANE):
-            slots = jnp.concatenate(
-                [got[l, q * pad : (q + 1) * pad, :] for l in range(local_count)]
-                + [jnp.zeros((SPAN - local_count * pad, width), bf16)],
-                axis=0,
-            )
-            for ref in refs:
-                total += jnp.dot(ref[block, pl.ds(q * SPAN, SPAN)], slots, preferred_element_type=f32)
-        return total
+        leave(pg_ref, pg_out, 3, l).start()
+
+    def combined(slots):
+        total = jnp.dot(sel[...], slots, preferred_element_type=f32)
+        return total.astype(bf16).reshape(line, row_total, width)
 
     def home(k):
         to = lax.rem(z + k, line)
@@ -390,8 +398,8 @@
     back(0)
     for l in range(local_count):
         swap_wait(o_send, o_got, o_ss, o_rs, l)
-    for j in range(line):
-        m_send[j] = combined(o_got, [whi, wmid], j).astype(bf16)
+    outs = o_got[...].reshape(lanes, width).astype(f32)
+    m_send[...] = combined((w_ref[:, :1] * outs).astype(bf16))
     for k in range(1, line):
         home(k).start()
     keep_mixed = pltpu.make_async_copy(m_send.at[z], m_got.at[z], m_rs.at[0])
@@ -400,17 +408,21 @@
         back(l)
     for l in range(local_count):
         swap_wait(d_send, d_got, d_ss, d_rs, l)
-    for j in range(line):
-        part_ref[j] = combined(d_got, [sel], j).astype(bf16)
+    part_ref[...] = combined(d_got[...].reshape(lanes, width))
     for k in range(1, line):
         home(k).wait()
     keep_mixed.wait()
     mixed_ref[...] = sum(m_got[j].astype(f32) for j in range(line)).astype(bf16)
     settle(rows_all, r_ss, r_rs)
     settle(cot_all, c_ss, c_rs)
-
-
-def plane_call(rows, cotangent, up_proj, down_proj, line, local_count, pad):
+    for l in range(local_count):
+        for n, (ref, out) in enumerate(
+            ((x_ref, x_out), (s_ref, s_out), (act_ref, act_out), (pg_ref, pg_out))
+        ):
+            leave(ref, out, n, l).wait()
+
+
+def plane_call(rows, places, cotangent, up_proj, down_proj, line, local_count, pad):
     bf16, f32 = jnp.bfloat16, jnp.float32
     row_total, width = cotangent.shape
     taken = PLANE * pad
@@ -418,7 +430,7 @@
     wide = (local_count, taken, FF)
     dma = pltpu.SemaphoreType.DMA
     vmem, anywhere = pl.BlockSpec(memory_space=pltpu.VMEM), pl.BlockSpec(memory_space=pl.ANY)
-    table = pltpu.VMEM((line * row_total, width), bf16)
+    lanes = local_count * taken
     blocks = (line, row_total, width)
     swaps = (local_count, PLANE)
     return pl.pallas_call(
@@ -431,26 +443,28 @@
             jax.ShapeDtypeStruct(wide, bf16),
             jax.ShapeDtypeStruct(wide, bf16),
         ],
-        in_specs=[vmem, vmem, anywhere, anywhere],
-        out_specs=[vmem] * 6,
+        in_specs=[vmem, vmem, vmem, anywhere, anywhere],
+        out_specs=[vmem] * 2 + [anywhere] * 4,
         scratch_shapes=[
-            pltpu.VMEM((line,) + rows.shape, bf16),
+            pltpu.VMEM((line, row_total + places.shape[0], width), bf16),
             pltpu.VMEM(blocks, bf16),
             pltpu.VMEM(up_proj.shape, bf16),
             pltpu.VMEM(down_proj.shape, bf16),
         ]
-        + [table] * 4
+        + [pltpu.VMEM((line * row_total, lanes), bf16), pltpu.VMEM((lanes, 128), f32)]
+        + [pltpu.VMEM(slots, bf16)] * 2
+        + [pltpu.VMEM(wide, bf16)] * 2
         + [pltpu.VMEM(slots, bf16)] * 6
         + [pltpu.VMEM(wide, f32), pltpu.VMEM((taken, width), f32)]
         + [pltpu.VMEM(blocks, bf16)] * 2
-        + [dma((2,)), dma((2,))]
+        + [dma((2,)), dma((3,)), dma((4, local_count))]
         + [dma((2, line)), dma((line,))] * 2
         + [dma(swaps)] * 8
         + [dma((line,))] * 2,
         compiler_params=pltpu.CompilerParams(
             collective_id=0, has_side_effects=True, vmem_limit_bytes=60 << 20
         ),
-    )(rows, cotangent, up_proj, down_proj)
+    )(rows, places, cotangent, up_proj, down_proj)
 
 
 def plane_plan(rows, cotangent, up_proj, down_proj, mix_weight, task_counts, expert_order):
@@ -465,7 +479,7 @@
         me, line, local_count, pad, row_total, width,
     )
     mixed, parts, inputs, scaled, act, pre_grad = plane_call(
-        jnp.concatenate([rows, places]), cotangent, up_proj, down_proj, line, local_count, pad
+        rows, places, cotangent, up_proj, down_proj, line, local_count, pad
     )
     groups = [[z * PLANE + p for z in range(line)] for p in range(PLANE)]
     home = lax.all_to_all(parts, "expert", 0, 0, axis_index_groups=groups, tiled=True)
@@ -479,8 +493,8 @@
     owners = lax.axis_size("expert")
     whole_experts = up_proj.shape[1] % FF == 0
     local_count = up_proj.shape[1] // FF
-    fits = owners % PLANE == 0 and local_count * (-(-owners // PLANE * CAP // 16) * 16) <= SPAN
-    wide_plane = fits and owners > PLANE and rows.shape[1] == PLANE * SPAN
+    fits = owners % PLANE == 0 and local_count * -(-owners // PLANE * CAP // 16) * 16 * PLANE <= rows.shape[1]
+    wide_plane = fits and owners > PLANE
     plan = plane_plan if whole_experts and wide_plane else direct_plan
     return plan(rows, cotangent, up_proj, *others)
 

time: 144 us -> 136 us (0.944)
  Pallas kernels: 122 us -> 116 us
  local copies, waits for them, and re-layouts: 5.41 us -> 2.51 us
    pallas_call x1, Pallas kernels: 101 us -> 95.4 us  [plane_call(): pl.pallas_call(functools.partial(plane_kernel, line, local_count, pad), o...]
    concatenate x1 -> x0, local copies, waits for them, and re-layouts: 2.9 us -> none  [plane_plan(): jnp.concatenate([rows, places])]
  transfers between devices with their start and end apart: 1 -> 1, of which waited for: 1 -> 1; matrix products, arithmetic and copies ran while one was open for 0% -> 0% of each run, Pallas kernels for 14% -> 15%
where the time goes in v2:
time: 136 us; the launch traced here: 135 us
  Pallas kernels  116 us (85%)
  waiting for transfers between devices  6.5 us (5%)
  starting transfers between devices  5.56 us (4%)
  other arithmetic  4.43 us (3%)
  local copies, waits for them, and re-layouts  2.51 us (2%)
    pallas_call x1, Pallas kernels, plane_call(): pl.pallas_call(functools.partial(plane_kernel, line, local_count, pad), o...  95.4 us
    pallas_call x1, Pallas kernels, down_grad_call(): pl.pallas_call(grad_kernel, grid=(local_count, units // tile), in_specs=[...  10.2 us
    pallas_call x1, Pallas kernels, up_grad_call(): pl.pallas_call(grad_kernel, grid=(local_count, units // tile), in_specs=[...  10.1 us
    all_to_all x1, waiting for transfers between devices, plane_plan(): lax.all_to_all(parts, 'expert', 0, 0, axis_index_groups=groups, tiled=True)  6.5 us
    all_to_all x1, starting transfers between devices, plane_plan(): lax.all_to_all(parts, 'expert', 0, 0, axis_index_groups=groups, tiled=True)  5.56 us
  transfers between devices with their start and end apart: 1, of which 1 were waited for; matrix products, arithmetic and copies ran while one was open for 0% of the time, Pallas kernels for 15%

profile of v2, /device:TPU:0, one launch (start us, length us, event | category | flops | bytes accessed | tf_op | source)
XLA Modules:
  0.0 135.4 jit_solution(7904341224609323050)
XLA Ops:
  0.7 0.8 select_reduce_fusion.6
  1.5 0.1 broadcast_in_dim.114
  1.6 0.1 broadcast_in_dim.115
  1.7 0.8 copy.13
  2.4 0.1 broadcast_in_dim.119
  2.5 0.7 broadcast_in_dim.106
  3.2 0.1 broadcast_in_dim.107
  3.3 0.8 select_reduce_fusion.3
  4.1 0.8 select_reduce_fusion.4
  4.8 0.1 multiply_add_fusion
  4.9 0.2 select_reduce_fusion
  5.1 0.2 select_reduce_fusion.1
  5.4 0.6 pad_maximum_fusion.places_ref
  6.0 95.4 %shard_map.102 = (bf16[128,1024]{1,0:T(8,128)(2,1)}, bf16[4,128,1024]{2,1,0:T(8,128)(2,1)}, bf16[2,320,1024]{2,1,0:T(8,128)(2,1)}, bf16[2,320,1024]{2,1,0:T(8,12...) custom-call(bf16[128,1024]{1,0:T(8,128)(2,1)} %rows_ref.1, ...), custom_call_target="tpu_custom_call" | custom-call | tf_op jit(solution)/shard_map/pallas_call | solution.py:436
  101.5 5.6 %all-to-all-start = ((bf16[4,128,1024]{2,1,0:T(8,128)(2,1)}), bf16[4,128,1024]{2,1,0:T(8,128)(2,1)S(1)}, u32[]{:S(2)}, u32[]{:S(2)}) async-start(bf16[4,128,1024]{2,1,0:T(8,128)(2,1)} %get-tuple-element.11), calls=%async_computation | async-start | bytes 2097152 | tf_op jit(solution)/shard_map/all_to_all | solution.py:485
  107.0 10.1 %shard_map.103 = bf16[1024,4096]{1,0:T(8,128)(2,1)} custom-call(bf16[2,320,1024]{2,1,0:T(8,128)(2,1)} %get-tuple-element.12.a_ref, bf16[2,320,2048]{2,1,0:T(8,128)(2,1)} %get-tuple-element.13.b_ref), custom_call_target="tpu_custom_call" | custom-call | flops 2684354560 | bytes 12320768 | tf_op jit(solution)/shard_map/pallas_call | solution.py:149
  117.1 0.0 copy-start
  117.1 10.2 %shard_map.104 = bf16[4096,1024]{1,0:T(8,128)(2,1)} custom-call(bf16[2,320,2048]{2,1,0:T(8,128)(2,1)} %get-tuple-element.14.a_ref, bf16[2,320,1024]{2,1,0:T(8,128)(2,1)} %get-tuple-element.15.b_ref), custom_call_target="tpu_custom_call" | custom-call | flops 2684354560 | bytes 12320768 | tf_op jit(solution)/shard_map/pallas_call | solution.py:166
  127.3 6.5 %all-to-all-done = bf16[4,128,1024]{2,1,0:T(8,128)(2,1)S(1)} async-done(((bf16[4,128,1024]{2,1,0:T(8,128)(2,1)}), bf16[4,128,1024]{2,1,0:T(8,128)(2,1)S(1)}, u32[]{:S(2)}, u32[]{:S(2)}) %all-to-all-start) | async-done | bytes 1048608 | tf_op jit(solution)/shard_map/all_to_all | solution.py:485
  133.8 0.9 reduce_sum.82
  134.7 0.0 copy-done
  134.7 0.7 copy.15
  (6 shorter events, 0.1 us)
Async XLA Ops:
  101.5 32.3 %all-to-all-start = ((bf16[4,128,1024]{2,1,0:T(8,128)(2,1)}), bf16[4,128,1024]{2,1,0:T(8,128)(2,1)S(1)}, u32[]{:S(2)}, u32[]{:S(2)}) async-start(bf16[4,128,1024]{2,1,0:T(8,128)(2,1)} %get-tuple-element.11), calls=%async_computation | async-start | bytes 2097152 | tf_op jit(solution)/shard_map/all_to_all | solution.py:485
  117.1 17.6 %copy-start = (bf16[128,1024]{1,0:T(8,128)(2,1)S(1)}, bf16[128,1024]{1,0:T(8,128)(2,1)}, u32[]{:S(2)}) copy-start(bf16[128,1024]{1,0:T(8,128)(2,1)} %get-tuple-element.31) | copy-start | bytes 786436

commit v3 on v2

--- a/solution.py
+++ b/solution.py
@@ -13,7 +13,7 @@
 K = 4
 CAP = 18
 PLANE = 4
-TILE = 512
+TILE = 1024
 
 
 def block_route(counts, expert_list, mix_flat, row_total):

time: 136 us -> 135 us (level)
  no operation moved by 1% of the time
where the time goes in v3:
time: 135 us
  Pallas kernels  115 us (85%)
  waiting for transfers between devices  6.5 us (5%)
  starting transfers between devices  5.56 us (4%)
  other arithmetic  4.43 us (3%)
  local copies, waits for them, and re-layouts  2.51 us (2%)
    pallas_call x1, Pallas kernels, plane_call(): pl.pallas_call(functools.partial(plane_kernel, line, local_count, pad), o...  94.6 us
    pallas_call x1, Pallas kernels, down_grad_call(): pl.pallas_call(grad_kernel, grid=(local_count, units // tile), in_specs=[...  10.2 us
    pallas_call x1, Pallas kernels, up_grad_call(): pl.pallas_call(grad_kernel, grid=(local_count, units // tile), in_specs=[...  10.1 us
    all_to_all x1, waiting for transfers between devices, plane_plan(): lax.all_to_all(parts, 'expert', 0, 0, axis_index_groups=groups, tiled=True)  6.5 us
    all_to_all x1, starting transfers between devices, plane_plan(): lax.all_to_all(parts, 'expert', 0, 0, axis_index_groups=groups, tiled=True)  5.56 us
  transfers between devices with their start and end apart: 1, of which 1 were waited for; matrix products, arithmetic and copies ran while one was open for 0% of the time, Pallas kernels for 15%

profile of v3, /device:TPU:0, one launch (start us, length us, event | category | flops | bytes accessed | tf_op | source)
XLA Modules:
  0.0 134.6 jit_solution(7439879980866085353)
XLA Ops:
  0.7 0.8 select_reduce_fusion.6
  1.5 0.1 broadcast_in_dim.114
  1.6 0.1 broadcast_in_dim.115
  1.7 0.8 copy.13
  2.4 0.1 broadcast_in_dim.119
  2.5 0.7 broadcast_in_dim.106
  3.2 0.1 broadcast_in_dim.107
  3.3 0.8 select_reduce_fusion.3
  4.1 0.8 select_reduce_fusion.4
  4.8 0.1 multiply_add_fusion
  4.9 0.2 select_reduce_fusion
  5.1 0.2 select_reduce_fusion.1
  5.4 0.6 pad_maximum_fusion.places_ref
  6.0 94.6 %shard_map.102 = (bf16[128,1024]{1,0:T(8,128)(2,1)}, bf16[4,128,1024]{2,1,0:T(8,128)(2,1)}, bf16[2,320,1024]{2,1,0:T(8,128)(2,1)}, bf16[2,320,1024]{2,1,0:T(8,12...) custom-call(bf16[128,1024]{1,0:T(8,128)(2,1)} %rows_ref.1, ...), custom_call_target="tpu_custom_call" | custom-call | tf_op jit(solution)/shard_map/pallas_call | solution.py:436
  100.6 5.6 %all-to-all-start = ((bf16[4,128,1024]{2,1,0:T(8,128)(2,1)}), bf16[4,128,1024]{2,1,0:T(8,128)(2,1)S(1)}, u32[]{:S(2)}, u32[]{:S(2)}) async-start(bf16[4,128,1024]{2,1,0:T(8,128)(2,1)} %get-tuple-element.11), calls=%async_computation | async-start | bytes 2097152 | tf_op jit(solution)/shard_map/all_to_all | solution.py:485
  106.1 10.1 %shard_map.103 = bf16[1024,4096]{1,0:T(8,128)(2,1)} custom-call(bf16[2,320,1024]{2,1,0:T(8,128)(2,1)} %get-tuple-element.12.a_ref, bf16[2,320,2048]{2,1,0:T(8,128)(2,1)} %get-tuple-element.13.b_ref), custom_call_target="tpu_custom_call" | custom-call | flops 2684354560 | bytes 12320768 | tf_op jit(solution)/shard_map/pallas_call | solution.py:149
  116.3 0.0 copy-start
  116.3 10.2 %shard_map.104 = bf16[4096,1024]{1,0:T(8,128)(2,1)} custom-call(bf16[2,320,2048]{2,1,0:T(8,128)(2,1)} %get-tuple-element.14.a_ref, bf16[2,320,1024]{2,1,0:T(8,128)(2,1)} %get-tuple-element.15.b_ref), custom_call_target="tpu_custom_call" | custom-call | flops 2684354560 | bytes 12320768 | tf_op jit(solution)/shard_map/pallas_call | solution.py:166
  126.4 6.5 %all-to-all-done = bf16[4,128,1024]{2,1,0:T(8,128)(2,1)S(1)} async-done(((bf16[4,128,1024]{2,1,0:T(8,128)(2,1)}), bf16[4,128,1024]{2,1,0:T(8,128)(2,1)S(1)}, u32[]{:S(2)}, u32[]{:S(2)}) %all-to-all-start) | async-done | bytes 1048608 | tf_op jit(solution)/shard_map/all_to_all | solution.py:485
  132.9 0.9 reduce_sum.82
  133.9 0.0 copy-done
  133.9 0.7 copy.15
  (6 shorter events, 0.1 us)
Async XLA Ops:
  100.6 32.4 %all-to-all-start = ((bf16[4,128,1024]{2,1,0:T(8,128)(2,1)}), bf16[4,128,1024]{2,1,0:T(8,128)(2,1)S(1)}, u32[]{:S(2)}, u32[]{:S(2)}) async-start(bf16[4,128,1024]{2,1,0:T(8,128)(2,1)} %get-tuple-element.11), calls=%async_computation | async-start | bytes 2097152 | tf_op jit(solution)/shard_map/all_to_all | solution.py:485
  116.3 17.6 %copy-start = (bf16[128,1024]{1,0:T(8,128)(2,1)S(1)}, bf16[128,1024]{1,0:T(8,128)(2,1)}, u32[]{:S(2)}) copy-start(bf16[128,1024]{1,0:T(8,128)(2,1)} %get-tuple-element.31) | copy-start | bytes 786436
